TPU v7x, 32 devices: a whole 2x2x4 slice. The times are simulated.
32 devices in a mesh: depth: 2 (over core), lat: 16 (over z, y, x).
Axes of the slice: x: 2, y: 2, z: 4, core: 2. Of those that a mesh axis runs over, the one named last changes fastest.
Arguments:
- fields: float32 [6, 96, 16, 512], P(None, 'lat', 'depth'), may hold values from -3 to 3
- material: int32 [96, 16, 512], P('lat', 'depth'), may hold values from 0 to 3
- source_mask: int32 [96, 16, 512], P('lat', 'depth'), may hold values 0 or 1
- eps_table: float32 [4], replicated, may hold values from 1 to 6
- kerr_table: float32 [4], replicated, may hold values from 0.3 to 3
Outputs:
- fields_out: float32 [6, 96, 16, 512], P(None, 'lat', 'depth')
- image: float32 [96, 8, 512], P('lat', None, 'depth')
Inputs may be any that keep to these rules, and one draw needn't show every extreme that they name: material indexes the tables.
All inputs are finite; a program needn't handle non-finite values. No bound on the sum of `source_mask` on one device may be relied on, other than what follows from the above.
Results may differ from a plain program's by a relative error of at most 0.0003.
Values sent between devices are 32-bit elements; how exact they have to be, the bound alone decides.
No kernel may reach another device: no remote copies, remote signals or barrier semaphores. Data moves between devices by JAX's collectives and lax.ppermute only.
A program may use at most 64 MiB of HBM per device.

v0:
```python
import math
import jax
import jax.numpy as jnp
from jax import lax
from jax.sharding import PartitionSpec as P

STEPS = 16
HALO_STEPS = 4
COURANT = 0.55
OMEGAS = (0.9, 1.3)
SOURCE_AMP = 1.0
QUARTERS = (3, 5)
HIGHEST = lax.Precision.HIGHEST


def padded_2(block, sides, width):
    for axis, dim in sides:
        count = lax.axis_size(axis)
        forward = [(i, i + 1) for i in range(count - 1)]
        backward = [(target, source) for source, target in forward]
        low = lax.ppermute(
            lax.slice_in_dim(block, block.shape[dim] - width, None, axis=dim), axis, forward
        )
        high = lax.ppermute(lax.slice_in_dim(block, 0, width, axis=dim), axis, backward)
        block = jnp.concatenate([low, block, high], axis=dim)
    return block


def from_root(block, axis, owner):
    block = jnp.where(lax.axis_index(axis) == owner, block, jnp.zeros_like(block))
    return lax.psum(block, axis)


def forward_diff(field, along):
    length = field.shape[along]
    ahead = lax.slice_in_dim(field, 1, length, axis=along)
    ahead = jnp.concatenate(
        [ahead, jnp.zeros_like(lax.slice_in_dim(field, 0, 1, axis=along))], axis=along
    )
    return ahead - field


def backward_diff(field, along):
    length = field.shape[along]
    behind = lax.slice_in_dim(field, 0, length - 1, axis=along)
    behind = jnp.concatenate(
        [jnp.zeros_like(lax.slice_in_dim(field, 0, 1, axis=along)), behind], axis=along
    )
    return field - behind


def drive(moment):
    middle = moment + 0.5
    return SOURCE_AMP * (jnp.sin(OMEGAS[0] * middle) + jnp.sin(OMEGAS[1] * middle))


def yee_step(fields, permittivity, kerr_coef, source_flag, inside, pulse):
    elec_x, elec_y, elec_z = (fields[0], fields[1], fields[2])
    magn_x, magn_y, magn_z = (fields[3], fields[4], fields[5])
    magn_x = (magn_x - COURANT * (forward_diff(elec_z, 2) - forward_diff(elec_y, 1))) * inside
    magn_y = (magn_y - COURANT * (forward_diff(elec_x, 1) - forward_diff(elec_z, 0))) * inside
    magn_z = (magn_z - COURANT * (forward_diff(elec_y, 0) - forward_diff(elec_x, 2))) * inside
    energy = elec_x * elec_x + elec_y * elec_y + elec_z * elec_z
    factor = COURANT / (permittivity + kerr_coef * energy)
    new_x = (
        elec_x
        + factor * (backward_diff(magn_z, 2) - backward_diff(magn_y, 1))
        + source_flag * pulse
    ) * inside
    new_y = (elec_y + factor * (backward_diff(magn_x, 1) - backward_diff(magn_z, 0))) * inside
    new_z = (elec_z + factor * (backward_diff(magn_y, 0) - backward_diff(magn_x, 2))) * inside
    return jnp.stack([new_x, new_y, new_z, magn_x, magn_y, magn_z])


def lookup(material, table):
    result = jnp.zeros(material.shape, jnp.float32)
    for level in range(table.shape[0]):
        result = jnp.where(material == level, table[level], result)
    return result


def accumulate(spectrum, plane, moment):
    later = moment + 1.0
    trig = jnp.stack(
        [jnp.stack([jnp.cos(omega * later), -jnp.sin(omega * later)]) for omega in OMEGAS]
    )
    return spectrum + trig[:, None, :, None, None] * plane[None, :, None, :, :]


def chirp(row_index, col_index, length):
    gap = row_index[:, None] - col_index[None, :]
    squared = gap * gap
    reals, imags = ([], [])
    for quarter in QUARTERS:
        wrapped = quarter * squared % (8 * length)
        phase = wrapped.astype(jnp.float32) * (math.pi / (4.0 * length))
        reals.append(jnp.cos(phase) / math.sqrt(length))
        imags.append(jnp.sin(phase) / math.sqrt(length))
    return (jnp.stack(reals), jnp.stack(imags))


def column_transform(real, imag, y_real, y_imag):
    v_real = jnp.einsum("fcxy,fyk->fcxk", real, y_real, precision=HIGHEST) - jnp.einsum(
        "fcxy,fyk->fcxk", imag, y_imag, precision=HIGHEST
    )
    v_imag = jnp.einsum("fcxy,fyk->fcxk", real, y_imag, precision=HIGHEST) + jnp.einsum(
        "fcxy,fyk->fcxk", imag, y_real, precision=HIGHEST
    )
    return (v_real, v_imag)


def row_transform(x_real, x_imag, v_real, v_imag):
    w_real = jnp.einsum("fix,fcxk->ifck", x_real, v_real, precision=HIGHEST) - jnp.einsum(
        "fix,fcxk->ifck", x_imag, v_imag, precision=HIGHEST
    )
    w_imag = jnp.einsum("fix,fcxk->ifck", x_real, v_imag, precision=HIGHEST) + jnp.einsum(
        "fix,fcxk->ifck", x_imag, v_real, precision=HIGHEST
    )
    return jnp.stack([w_real, w_imag], axis=3)


def local(fields, material, source_mask, eps_table, kerr_table):
    width_x = fields.shape[1]
    depth_z = fields.shape[2]
    span_y = fields.shape[3]
    lat_count = lax.axis_size("lat")
    depth_count = lax.axis_size("depth")
    total_x = width_x * lat_count
    total_z = depth_z * depth_count
    lat_pos = lax.axis_index("lat")
    depth_pos = lax.axis_index("depth")
    coefs = jnp.stack(
        [lookup(material, eps_table), lookup(material, kerr_table), source_mask.astype(jnp.float32)]
    )
    empty_spectrum = jnp.zeros((2, 2, 2, width_x, span_y), jnp.float32)
    coef_pad = padded_2(coefs, (("depth", 2), ("lat", 1)), HALO_STEPS)
    place_x = lat_pos * width_x - HALO_STEPS + jnp.arange(width_x + 2 * HALO_STEPS, dtype=jnp.int32)
    place_z = (
        depth_pos * depth_z - HALO_STEPS + jnp.arange(depth_z + 2 * HALO_STEPS, dtype=jnp.int32)
    )
    valid_x = (place_x >= 0) & (place_x < total_x)
    valid_z = (place_z >= 0) & (place_z < total_z)
    valid = valid_x[:, None] & valid_z[None, :]
    setup_inside = valid.astype(jnp.float32)[:, :, None]
    setup_permittivity = jnp.where(valid[:, :, None], coef_pad[0], 1.0)
    kerr_coef = coef_pad[1]
    source_flag = coef_pad[2]

    def one_block(block, carry):
        state, spectrum = carry
        padded = padded_2(state, (("depth", 2), ("lat", 1)), HALO_STEPS)
        for inner in range(HALO_STEPS):
            moment = (block * HALO_STEPS + inner).astype(jnp.float32)
            padded = yee_step(
                padded, setup_permittivity, kerr_coef, source_flag, setup_inside, drive(moment)
            )
            plane = padded[0:2, HALO_STEPS : HALO_STEPS + width_x, HALO_STEPS + depth_z - 1, :]
            spectrum = accumulate(spectrum, plane, moment)
        state = padded[:, HALO_STEPS : HALO_STEPS + width_x, HALO_STEPS : HALO_STEPS + depth_z]
        return (state, spectrum)

    state, spectrum = lax.fori_loop(0, STEPS // HALO_STEPS, one_block, (fields, empty_spectrum))
    spectrum = from_root(spectrum, "depth", depth_count - 1)
    col_count = span_y // depth_count
    col_index = depth_pos * col_count + jnp.arange(col_count, dtype=jnp.int32)
    y_real, y_imag = chirp(jnp.arange(span_y, dtype=jnp.int32), col_index, span_y)
    v_real, v_imag = column_transform(spectrum[:, :, 0], spectrum[:, :, 1], y_real, y_imag)
    row_local = lat_pos * width_x + jnp.arange(width_x, dtype=jnp.int32)
    row_index = jnp.arange(width_x * lax.axis_size("lat"), dtype=jnp.int32)
    x_real, x_imag = chirp(row_index, row_local, total_x)
    image = lax.psum_scatter(
        row_transform(x_real, x_imag, v_real, v_imag), "lat", scatter_dimension=0, tiled=True
    )
    return (state, image.reshape(width_x, 8, col_count))


def solution(mesh):
    placed = (
        P(None, "lat", "depth", None),
        P("lat", "depth", None),
        P("lat", "depth", None),
        P(),
        P(),
    )
    return jax.shard_map(
        local,
        mesh=mesh,
        in_specs=placed,
        out_specs=(P(None, "lat", "depth", None), P("lat", None, "depth")),
        check_vma=False,
    )
```

profile of v0, /device:TPU:0, one launch (start us, length us, event | category | flops | bytes accessed | tf_op | source)
XLA Modules:
  0.0 429.3 jit_solution(4723124953728280105)
XLA Ops:
  11.0 3.4 select_bitcast_fusion.1
  14.5 2.5 select_bitcast_fusion
  17.0 2.4 collective-permute-start.4
  20.9 1.8 collective-permute-done.5
  22.9 4.2 collective-permute-start.6
  29.0 5.1 %cosine_multiply_fusion.1 = (f32[1,512,256]{2,1,0:T(8,128)}, f32[1,512,256]{2,1,0:T(8,128)}, f32[1,512,256]{2,1,0:T(8,128)}, f32[1,512,256]{2,1,0:T(8,128)}) fusion(s32[256]{0:T(256)S(1)} %iota_add_fusion), kind=kLoop, calls=%fused_computation.100 | loop fusion | flops 4456448 | bytes 2098176 | tf_op jit(solution)/shard_map/div | solution.py:97
  34.1 10.1 %collective-permute-done.6 = f32[3,4,16,512]{3,2,1,0:T(8,128)S(1)} collective-permute-done((f32[3,4,16,512]{3,2,1,0:T(8,128)S(1)}, f32[3,4,16,512]{3,2,1,0:T(8,128)S(1)}, u32[]{:S(2)}, u32[]{:S(2)}) %collective-permute-start.6) | collective-permute-done | bytes 393248 | tf_op jit(solution)/shard_map/ppermute | solution.py:21
  44.2 1.9 collective-permute-done.7
  46.6 234.1 %while.16 = (s32[]{:T(128)}, f32[6,6,8,512]{3,2,1,0:T(8,128)S(1)}, f32[2,2,2,6,512]{4,3,2,1,0:T(8,128)S(1)}, f32[14,16,512]{2,1,0:T(8,128)S(1)}, f32[14,16,512]{...) while((s32[]{:T(128)}, f32[6,6,8,512]{3,2,1,0:T(8,128)S(1)}, ...), condition=%wide.region_1.2_spmd.clone, body=%wide.region_0.1_spmd.clone.sunk | while | flops 24691188 | bytes 132281024 | solution.py:162
  48.2 3.1 collective-permute-start.1
  55.3 5.5 %collective-permute-start.3 = (f32[6,4,16,512]{3,2,1,0:T(8,128)S(1)}, f32[6,4,16,512]{3,2,1,0:T(8,128)}, u32[]{:S(2)}, u32[]{:S(2)}) collective-permute-start(f32[6,4,16,512]{3,2,1,0:T(8,128)S(1)} %get-tuple-element.357), channel_id=1, source_target_pairs={{0,1},{1,2},{2,3},{3,4},{4,5},{5,6},{6,7},{7,8},{8,9},{9,10},{10,1... | collective-permute-start | bytes 2359304 | tf_op jit(solution)/shard_map/while/body/eval_jaxpr/ppermute | solution.py:21
  61.6 15.0 %collective-permute-done.2 = f32[6,4,16,512]{3,2,1,0:T(8,128)} collective-permute-done((f32[6,4,16,512]{3,2,1,0:T(8,128)}, f32[6,4,16,512]{3,2,1,0:T(8,128)}, u32[]{:S(2)}, u32[]{:S(2)}) %collective-permute-start.2) | collective-permute-done | bytes 786464 | tf_op jit(solution)/shard_map/while/body/eval_jaxpr/ppermute | solution.py:24
  76.6 14.7 %collective-permute-done.3 = f32[6,4,16,512]{3,2,1,0:T(8,128)} collective-permute-done((f32[6,4,16,512]{3,2,1,0:T(8,128)S(1)}, f32[6,4,16,512]{3,2,1,0:T(8,128)}, u32[]{:S(2)}, u32[]{:S(2)}) %collective-permute-start.3) | collective-permute-done | bytes 786464 | tf_op jit(solution)/shard_map/while/body/eval_jaxpr/ppermute | solution.py:21
  91.3 1.8 pad_maximum_fusion.25
  104.8 3.1 collective-permute-start.1
  111.9 6.0 %collective-permute-start.3 = (f32[6,4,16,512]{3,2,1,0:T(8,128)S(1)}, f32[6,4,16,512]{3,2,1,0:T(8,128)}, u32[]{:S(2)}, u32[]{:S(2)}) collective-permute-start(f32[6,4,16,512]{3,2,1,0:T(8,128)S(1)} %get-tuple-element.357), channel_id=1, source_target_pairs={{0,1},{1,2},{2,3},{3,4},{4,5},{5,6},{6,7},{7,8},{8,9},{9,10},{10,1... | collective-permute-start | bytes 2359304 | tf_op jit(solution)/shard_map/while/body/eval_jaxpr/ppermute | solution.py:21
  118.9 15.0 %collective-permute-done.2 = f32[6,4,16,512]{3,2,1,0:T(8,128)} collective-permute-done((f32[6,4,16,512]{3,2,1,0:T(8,128)}, f32[6,4,16,512]{3,2,1,0:T(8,128)}, u32[]{:S(2)}, u32[]{:S(2)}) %collective-permute-start.2) | collective-permute-done | bytes 786464 | tf_op jit(solution)/shard_map/while/body/eval_jaxpr/ppermute | solution.py:24
  133.8 17.1 %collective-permute-done.3 = f32[6,4,16,512]{3,2,1,0:T(8,128)} collective-permute-done((f32[6,4,16,512]{3,2,1,0:T(8,128)S(1)}, f32[6,4,16,512]{3,2,1,0:T(8,128)}, u32[]{:S(2)}, u32[]{:S(2)}) %collective-permute-start.3) | collective-permute-done | bytes 786464 | tf_op jit(solution)/shard_map/while/body/eval_jaxpr/ppermute | solution.py:21
  151.0 1.8 pad_maximum_fusion.25
  164.5 3.1 collective-permute-start.1
  171.6 6.0 %collective-permute-start.3 = (f32[6,4,16,512]{3,2,1,0:T(8,128)S(1)}, f32[6,4,16,512]{3,2,1,0:T(8,128)}, u32[]{:S(2)}, u32[]{:S(2)}) collective-permute-start(f32[6,4,16,512]{3,2,1,0:T(8,128)S(1)} %get-tuple-element.357), channel_id=1, source_target_pairs={{0,1},{1,2},{2,3},{3,4},{4,5},{5,6},{6,7},{7,8},{8,9},{9,10},{10,1... | collective-permute-start | bytes 2359304 | tf_op jit(solution)/shard_map/while/body/eval_jaxpr/ppermute | solution.py:21
  178.5 15.0 %collective-permute-done.2 = f32[6,4,16,512]{3,2,1,0:T(8,128)} collective-permute-done((f32[6,4,16,512]{3,2,1,0:T(8,128)}, f32[6,4,16,512]{3,2,1,0:T(8,128)}, u32[]{:S(2)}, u32[]{:S(2)}) %collective-permute-start.2) | collective-permute-done | bytes 786464 | tf_op jit(solution)/shard_map/while/body/eval_jaxpr/ppermute | solution.py:24
  193.5 15.5 %collective-permute-done.3 = f32[6,4,16,512]{3,2,1,0:T(8,128)} collective-permute-done((f32[6,4,16,512]{3,2,1,0:T(8,128)S(1)}, f32[6,4,16,512]{3,2,1,0:T(8,128)}, u32[]{:S(2)}, u32[]{:S(2)}) %collective-permute-start.3) | collective-permute-done | bytes 786464 | tf_op jit(solution)/shard_map/while/body/eval_jaxpr/ppermute | solution.py:21
  209.0 1.8 pad_maximum_fusion.25
  222.5 3.1 collective-permute-start.1
  229.6 6.0 %collective-permute-start.3 = (f32[6,4,16,512]{3,2,1,0:T(8,128)S(1)}, f32[6,4,16,512]{3,2,1,0:T(8,128)}, u32[]{:S(2)}, u32[]{:S(2)}) collective-permute-start(f32[6,4,16,512]{3,2,1,0:T(8,128)S(1)} %get-tuple-element.357), channel_id=1, source_target_pairs={{0,1},{1,2},{2,3},{3,4},{4,5},{5,6},{6,7},{7,8},{8,9},{9,10},{10,1... | collective-permute-start | bytes 2359304 | tf_op jit(solution)/shard_map/while/body/eval_jaxpr/ppermute | solution.py:21
  236.5 15.0 %collective-permute-done.2 = f32[6,4,16,512]{3,2,1,0:T(8,128)} collective-permute-done((f32[6,4,16,512]{3,2,1,0:T(8,128)}, f32[6,4,16,512]{3,2,1,0:T(8,128)}, u32[]{:S(2)}, u32[]{:S(2)}) %collective-permute-start.2) | collective-permute-done | bytes 786464 | tf_op jit(solution)/shard_map/while/body/eval_jaxpr/ppermute | solution.py:24
  251.5 17.1 %collective-permute-done.3 = f32[6,4,16,512]{3,2,1,0:T(8,128)} collective-permute-done((f32[6,4,16,512]{3,2,1,0:T(8,128)S(1)}, f32[6,4,16,512]{3,2,1,0:T(8,128)}, u32[]{:S(2)}, u32[]{:S(2)}) %collective-permute-start.3) | collective-permute-done | bytes 786464 | tf_op jit(solution)/shard_map/while/body/eval_jaxpr/ppermute | solution.py:21
  281.9 18.3 %all-reduce.52.cloned.1.call-done = f32[2,2,2,6,512]{4,3,1,0,2:T(8,128)} async-done(((f32[2,2,2,6,512]{4,3,1,0,2:T(8,128)}), f32[2,2,2,6,512]{4,3,1,0,2:T(8,128)}) %all-reduce.52.cloned.1.call-update) | async-done | bytes 98320 | tf_op jit(solution)/shard_map/psum | solution.py:31
  300.2 1.9 fusion.13
  302.1 1.9 convolution_add_fusion.1
  310.2 110.9 %all-reduce.54.cloned.1.call-done = f32[96,2,2,2,256]{4,3,2,1,0:T(2,128)} async-done(((f32[96,2,2,2,256]{4,3,2,1,0:T(2,128)}), f32[96,2,2,2,256]{4,3,2,1,0:T(2,128)}) %all-reduce.54.cloned.1.call-update) | async-done | bytes 786448
  (367 shorter events, 74.7 us)
Async XLA Ops:
  7.2 293.0 %all-reduce.52.cloned.1.call-start = ((), (), s32[]{:S(2)}) async-start(), calls=%async_computation | async-start | bytes 262144 | tf_op jit(solution)/shard_map/psum | solution.py:31
  17.0 3.8 collective-permute-start.4
  19.4 3.3 collective-permute-start.5
  22.9 21.3 %collective-permute-start.6 = (f32[3,4,16,512]{3,2,1,0:T(8,128)S(1)}, f32[3,4,16,512]{3,2,1,0:T(8,128)S(1)}, u32[]{:S(2)}, u32[]{:S(2)}) collective-permute-start(f32[3,4,16,512]{3,2,1,0:T(8,128)S(1)} %get-tuple-element.239), channel_id=1, source_target_pairs={{0,1},{1,2},{2,3},{3,4},{4,5},{5,6},{6,7},{7,8},{8,9},{9,10},{10,1... | collective-permute-start | bytes 1179656 | tf_op jit(solution)/shard_map/ppermute | solution.py:21
  27.1 19.0 %collective-permute-start.7 = (f32[3,4,16,512]{3,2,1,0:T(8,128)S(1)}, f32[3,4,16,512]{3,2,1,0:T(8,128)S(1)}, u32[]{:S(2)}, u32[]{:S(2)}) collective-permute-start(f32[3,4,16,512]{3,2,1,0:T(8,128)S(1)} %get-tuple-element.240), channel_id=1, source_target_pairs={{1,0},{2,1},{3,2},{4,3},{5,4},{6,5},{7,6},{8,7},{9,8},{10,9},{11,1... | collective-permute-start | bytes 1179656 | tf_op jit(solution)/shard_map/ppermute | solution.py:24
  34.1 12.4 %copy-start.1 = (f32[6,6,8,512]{3,2,1,0:T(8,128)S(1)}, f32[6,6,8,512]{3,2,1,0:T(8,128)}, u32[]{:S(2)}) copy-start(f32[6,6,8,512]{3,2,1,0:T(8,128)} %param.7) | copy-start | bytes 1769476
  46.6 235.2 %copy-start.7 = (s32[6]{0:T(128)S(1)}, s32[6]{0:T(128)}, u32[]{:S(2)}) copy-start(s32[6]{0:T(128)} %iota_add_fusion.1) | copy-start | bytes 76
  46.9 5.8 %collective-permute-start = (f32[6,6,4,512]{3,2,1,0:T(4,128)S(1)}, f32[6,6,4,512]{3,2,1,0:T(4,128)S(1)}, u32[]{:S(2)}, u32[]{:S(2)}) collective-permute-start(f32[6,6,4,512]{3,2,1,0:T(4,128)S(1)} %get-tuple-element.354), channel_id=1, source_target_pairs={{16,0},{17,1},{18,2},{19,3},{20,4},{21,5},{22,6},{23,7},{24,8},{25... | collective-permute-start | bytes 884744 | tf_op jit(solution)/shard_map/while/body/eval_jaxpr/ppermute | solution.py:24
  48.2 4.5 %collective-permute-start.1 = (f32[6,6,4,512]{3,2,1,0:T(4,128)S(1)}, f32[6,6,4,512]{3,2,1,0:T(4,128)S(1)}, u32[]{:S(2)}, u32[]{:S(2)}) collective-permute-start(f32[6,6,4,512]{3,2,1,0:T(4,128)S(1)} %get-tuple-element.355), channel_id=1, source_target_pairs={{0,16},{1,17},{2,18},{3,19},{4,20},{5,21},{6,22},{7,23},{8,24},{9,... | collective-permute-start | bytes 884744 | tf_op jit(solution)/shard_map/while/body/eval_jaxpr/ppermute | solution.py:21
  54.0 22.6 %collective-permute-start.2 = (f32[6,4,16,512]{3,2,1,0:T(8,128)}, f32[6,4,16,512]{3,2,1,0:T(8,128)}, u32[]{:S(2)}, u32[]{:S(2)}) collective-permute-start(f32[6,4,16,512]{3,2,1,0:T(8,128)} %get-tuple-element.356), channel_id=1, source_target_pairs={{1,0},{2,1},{3,2},{4,3},{5,4},{6,5},{7,6},{8,7},{9,8},{10,9},{11,1... | collective-permute-start | bytes 2359304 | tf_op jit(solution)/shard_map/while/body/eval_jaxpr/ppermute | solution.py:24
  55.3 36.0 %collective-permute-start.3 = (f32[6,4,16,512]{3,2,1,0:T(8,128)S(1)}, f32[6,4,16,512]{3,2,1,0:T(8,128)}, u32[]{:S(2)}, u32[]{:S(2)}) collective-permute-start(f32[6,4,16,512]{3,2,1,0:T(8,128)S(1)} %get-tuple-element.357), channel_id=1, source_target_pairs={{0,1},{1,2},{2,3},{3,4},{4,5},{5,6},{6,7},{7,8},{8,9},{9,10},{10,1... | collective-permute-start | bytes 2359304 | tf_op jit(solution)/shard_map/while/body/eval_jaxpr/ppermute | solution.py:21
  103.5 5.8 %collective-permute-start = (f32[6,6,4,512]{3,2,1,0:T(4,128)S(1)}, f32[6,6,4,512]{3,2,1,0:T(4,128)S(1)}, u32[]{:S(2)}, u32[]{:S(2)}) collective-permute-start(f32[6,6,4,512]{3,2,1,0:T(4,128)S(1)} %get-tuple-element.354), channel_id=1, source_target_pairs={{16,0},{17,1},{18,2},{19,3},{20,4},{21,5},{22,6},{23,7},{24,8},{25... | collective-permute-start | bytes 884744 | tf_op jit(solution)/shard_map/while/body/eval_jaxpr/ppermute | solution.py:24
  104.8 4.5 %collective-permute-start.1 = (f32[6,6,4,512]{3,2,1,0:T(4,128)S(1)}, f32[6,6,4,512]{3,2,1,0:T(4,128)S(1)}, u32[]{:S(2)}, u32[]{:S(2)}) collective-permute-start(f32[6,6,4,512]{3,2,1,0:T(4,128)S(1)} %get-tuple-element.355), channel_id=1, source_target_pairs={{0,16},{1,17},{2,18},{3,19},{4,20},{5,21},{6,22},{7,23},{8,24},{9,... | collective-permute-start | bytes 884744 | tf_op jit(solution)/shard_map/while/body/eval_jaxpr/ppermute | solution.py:21
  110.6 23.2 %collective-permute-start.2 = (f32[6,4,16,512]{3,2,1,0:T(8,128)}, f32[6,4,16,512]{3,2,1,0:T(8,128)}, u32[]{:S(2)}, u32[]{:S(2)}) collective-permute-start(f32[6,4,16,512]{3,2,1,0:T(8,128)} %get-tuple-element.356), channel_id=1, source_target_pairs={{1,0},{2,1},{3,2},{4,3},{5,4},{6,5},{7,6},{8,7},{9,8},{10,9},{11,1... | collective-permute-start | bytes 2359304 | tf_op jit(solution)/shard_map/while/body/eval_jaxpr/ppermute | solution.py:24
  111.9 39.0 %collective-permute-start.3 = (f32[6,4,16,512]{3,2,1,0:T(8,128)S(1)}, f32[6,4,16,512]{3,2,1,0:T(8,128)}, u32[]{:S(2)}, u32[]{:S(2)}) collective-permute-start(f32[6,4,16,512]{3,2,1,0:T(8,128)S(1)} %get-tuple-element.357), channel_id=1, source_target_pairs={{0,1},{1,2},{2,3},{3,4},{4,5},{5,6},{6,7},{7,8},{8,9},{9,10},{10,1... | collective-permute-start | bytes 2359304 | tf_op jit(solution)/shard_map/while/body/eval_jaxpr/ppermute | solution.py:21
  163.2 5.8 %collective-permute-start = (f32[6,6,4,512]{3,2,1,0:T(4,128)S(1)}, f32[6,6,4,512]{3,2,1,0:T(4,128)S(1)}, u32[]{:S(2)}, u32[]{:S(2)}) collective-permute-start(f32[6,6,4,512]{3,2,1,0:T(4,128)S(1)} %get-tuple-element.354), channel_id=1, source_target_pairs={{16,0},{17,1},{18,2},{19,3},{20,4},{21,5},{22,6},{23,7},{24,8},{25... | collective-permute-start | bytes 884744 | tf_op jit(solution)/shard_map/while/body/eval_jaxpr/ppermute | solution.py:24
  164.5 4.5 %collective-permute-start.1 = (f32[6,6,4,512]{3,2,1,0:T(4,128)S(1)}, f32[6,6,4,512]{3,2,1,0:T(4,128)S(1)}, u32[]{:S(2)}, u32[]{:S(2)}) collective-permute-start(f32[6,6,4,512]{3,2,1,0:T(4,128)S(1)} %get-tuple-element.355), channel_id=1, source_target_pairs={{0,16},{1,17},{2,18},{3,19},{4,20},{5,21},{6,22},{7,23},{8,24},{9,... | collective-permute-start | bytes 884744 | tf_op jit(solution)/shard_map/while/body/eval_jaxpr/ppermute | solution.py:21
  170.3 23.2 %collective-permute-start.2 = (f32[6,4,16,512]{3,2,1,0:T(8,128)}, f32[6,4,16,512]{3,2,1,0:T(8,128)}, u32[]{:S(2)}, u32[]{:S(2)}) collective-permute-start(f32[6,4,16,512]{3,2,1,0:T(8,128)} %get-tuple-element.356), channel_id=1, source_target_pairs={{1,0},{2,1},{3,2},{4,3},{5,4},{6,5},{7,6},{8,7},{9,8},{10,9},{11,1... | collective-permute-start | bytes 2359304 | tf_op jit(solution)/shard_map/while/body/eval_jaxpr/ppermute | solution.py:24
  171.6 37.4 %collective-permute-start.3 = (f32[6,4,16,512]{3,2,1,0:T(8,128)S(1)}, f32[6,4,16,512]{3,2,1,0:T(8,128)}, u32[]{:S(2)}, u32[]{:S(2)}) collective-permute-start(f32[6,4,16,512]{3,2,1,0:T(8,128)S(1)} %get-tuple-element.357), channel_id=1, source_target_pairs={{0,1},{1,2},{2,3},{3,4},{4,5},{5,6},{6,7},{7,8},{8,9},{9,10},{10,1... | collective-permute-start | bytes 2359304 | tf_op jit(solution)/shard_map/while/body/eval_jaxpr/ppermute | solution.py:21
  221.2 5.8 %collective-permute-start = (f32[6,6,4,512]{3,2,1,0:T(4,128)S(1)}, f32[6,6,4,512]{3,2,1,0:T(4,128)S(1)}, u32[]{:S(2)}, u32[]{:S(2)}) collective-permute-start(f32[6,6,4,512]{3,2,1,0:T(4,128)S(1)} %get-tuple-element.354), channel_id=1, source_target_pairs={{16,0},{17,1},{18,2},{19,3},{20,4},{21,5},{22,6},{23,7},{24,8},{25... | collective-permute-start | bytes 884744 | tf_op jit(solution)/shard_map/while/body/eval_jaxpr/ppermute | solution.py:24
  222.5 4.5 %collective-permute-start.1 = (f32[6,6,4,512]{3,2,1,0:T(4,128)S(1)}, f32[6,6,4,512]{3,2,1,0:T(4,128)S(1)}, u32[]{:S(2)}, u32[]{:S(2)}) collective-permute-start(f32[6,6,4,512]{3,2,1,0:T(4,128)S(1)} %get-tuple-element.355), channel_id=1, source_target_pairs={{0,16},{1,17},{2,18},{3,19},{4,20},{5,21},{6,22},{7,23},{8,24},{9,... | collective-permute-start | bytes 884744 | tf_op jit(solution)/shard_map/while/body/eval_jaxpr/ppermute | solution.py:21
  228.3 23.2 %collective-permute-start.2 = (f32[6,4,16,512]{3,2,1,0:T(8,128)}, f32[6,4,16,512]{3,2,1,0:T(8,128)}, u32[]{:S(2)}, u32[]{:S(2)}) collective-permute-start(f32[6,4,16,512]{3,2,1,0:T(8,128)} %get-tuple-element.356), channel_id=1, source_target_pairs={{1,0},{2,1},{3,2},{4,3},{5,4},{6,5},{7,6},{8,7},{9,8},{10,9},{11,1... | collective-permute-start | bytes 2359304 | tf_op jit(solution)/shard_map/while/body/eval_jaxpr/ppermute | solution.py:24
  229.6 39.0 %collective-permute-start.3 = (f32[6,4,16,512]{3,2,1,0:T(8,128)S(1)}, f32[6,4,16,512]{3,2,1,0:T(8,128)}, u32[]{:S(2)}, u32[]{:S(2)}) collective-permute-start(f32[6,4,16,512]{3,2,1,0:T(8,128)S(1)} %get-tuple-element.357), channel_id=1, source_target_pairs={{0,1},{1,2},{2,3},{3,4},{4,5},{5,6},{6,7},{7,8},{8,9},{9,10},{10,1... | collective-permute-start | bytes 2359304 | tf_op jit(solution)/shard_map/while/body/eval_jaxpr/ppermute | solution.py:21
  280.7 25.1 %copy-start = (f32[6,6,8,512]{3,2,1,0:T(8,128)}, f32[6,6,8,512]{3,2,1,0:T(8,128)S(1)}, u32[]{:S(2)}) copy-start(f32[6,6,8,512]{3,2,1,0:T(8,128)S(1)} %get-tuple-element.168) | copy-start | bytes 1769476
  280.7 23.7 %copy-start.4 = (f32[1,512,256]{2,1,0:T(8,128)S(1)}, f32[1,512,256]{2,1,0:T(8,128)}, u32[]{:S(2)}) copy-start(f32[1,512,256]{2,1,0:T(8,128)} %get-tuple-element.243) | copy-start | bytes 1572868
  280.7 23.7 %copy-start.5 = (f32[1,512,256]{2,1,0:T(8,128)S(1)}, f32[1,512,256]{2,1,0:T(8,128)}, u32[]{:S(2)}) copy-start(f32[1,512,256]{2,1,0:T(8,128)} %get-tuple-element.244) | copy-start | bytes 1572868
  280.8 24.4 %copy-start.2 = (f32[1,512,256]{2,1,0:T(8,128)S(1)}, f32[1,512,256]{2,1,0:T(8,128)}, u32[]{:S(2)}) copy-start(f32[1,512,256]{2,1,0:T(8,128)} %get-tuple-element.245) | copy-start | bytes 1572868
  280.8 24.4 %copy-start.3 = (f32[1,512,256]{2,1,0:T(8,128)S(1)}, f32[1,512,256]{2,1,0:T(8,128)}, u32[]{:S(2)}) copy-start(f32[1,512,256]{2,1,0:T(8,128)} %get-tuple-element.246) | copy-start | bytes 1572868
  281.5 139.6 %all-reduce.54.cloned.1.call-start = ((), (), s32[]{:S(2)}) async-start(), calls=%async_computation.1 | async-start | bytes 1572864
  300.2 4.3 %copy-start.6 = (f32[2,2,2,6,512]{4,3,1,0,2:T(8,128)S(1)}, f32[2,2,2,6,512]{4,3,1,0,2:T(8,128)}, u32[]{:S(2)}) copy-start(f32[2,2,2,6,512]{4,3,1,0,2:T(8,128)} %all-reduce.52.cloned.1.call-done) | copy-start | bytes 294916
  306.3 2.6 copy-start.8
Sparse Core Ops, SparseCore 0:
  281.6 18.5 all-reduce.51
  309.0 111.9 all-reduce.53
where the time goes:
time: 430 us; the launch traced here: 429 us
  waiting for transfers between devices  267 us (62%)
  starting transfers between devices  55.6 us (13%)
  other arithmetic  52 us (12%)
  local copies, waits for them, and re-layouts  22.5 us (5%)
  between operations  15 us (3%)
  loops' own time  9.67 us (2%)
  matrix products  7.03 us (2%)
    unnamed x3, waiting for transfers between devices  111 us
    ppermute x10, waiting for transfers between devices, padded_2(): lax.ppermute(lax.slice_in_dim(block, block.shape[dim] - width, None, axis...  74.6 us
    ppermute x10, waiting for transfers between devices, padded_2(): lax.ppermute(lax.slice_in_dim(block, 0, width, axis=dim), axis, backward)  63.6 us
    ppermute x10, starting transfers between devices, padded_2(): lax.ppermute(lax.slice_in_dim(block, block.shape[dim] - width, None, axis...  42.4 us
    psum x1, waiting for transfers between devices, from_root(): return lax.psum(block, axis)  18.3 us
    ppermute x10, starting transfers between devices, padded_2(): lax.ppermute(lax.slice_in_dim(block, 0, width, axis=dim), axis, backward)  12.9 us
    another operation x1, loops' own time, local(): lax.fori_loop(0, STEPS // HALO_STEPS, one_block, (fields, empty_spectrum))  9.67 us
    mul x12, other arithmetic, yee_step(): (elec_y + factor * (backward_diff(magn_x, 1) - backward_diff(magn_z, 0)))...  8.82 us
  transfers between devices with their start and end apart: 22, of which 13 were waited for; matrix products, arithmetic and copies ran while one was open for 2% of the time, Pallas kernels for 0%

commit v1 on v0

--- a/solution.py
+++ b/solution.py
@@ -11,6 +11,10 @@
 SOURCE_AMP = 1.0
 QUARTERS = (3, 5)
 HIGHEST = lax.Precision.HIGHEST
+
+
+def groups_solve(raw, comm_axis):
+    return jnp.sum(lax.all_gather(raw, comm_axis), axis=0)
 
 
 def padded_2(block, sides, width):
@@ -28,7 +32,7 @@
 
 def from_root(block, axis, owner):
     block = jnp.where(lax.axis_index(axis) == owner, block, jnp.zeros_like(block))
-    return lax.psum(block, axis)
+    return groups_solve(block, axis)
 
 
 def forward_diff(field, along):

time: 430 us -> 413 us (0.960)
  waiting for transfers between devices: 267 us -> 248 us
    psum x1 -> x0, waiting for transfers between devices: 18.3 us -> none  [from_root(): return lax.psum(block, axis)]
    unnamed x3 -> x2, waiting for transfers between devices: 111 us -> 110 us
  transfers between devices with their start and end apart: 22 -> 21, of which waited for: 13 -> 12; matrix products, arithmetic and copies ran while one was open for 2% -> 2% of each run, Pallas kernels for 0% -> 0%
where the time goes in v1:
time: 413 us; the launch traced here: 412 us
  waiting for transfers between devices  248 us (60%)
  starting transfers between devices  55.4 us (13%)
  other arithmetic  51.6 us (12%)
  local copies, waits for them, and re-layouts  22.6 us (5%)
  between operations  15.1 us (4%)
  loops' own time  9.68 us (2%)
  matrix products  6.96 us (2%)
    unnamed x2, waiting for transfers between devices  110 us
    ppermute x10, waiting for transfers between devices, padded_2(): lax.ppermute(lax.slice_in_dim(block, block.shape[dim] - width, None, axis...  75.1 us
    ppermute x10, waiting for transfers between devices, padded_2(): lax.ppermute(lax.slice_in_dim(block, 0, width, axis=dim), axis, backward)  63 us
    ppermute x10, starting transfers between devices, padded_2(): lax.ppermute(lax.slice_in_dim(block, block.shape[dim] - width, None, axis...  42.4 us
    ppermute x10, starting transfers between devices, padded_2(): lax.ppermute(lax.slice_in_dim(block, 0, width, axis=dim), axis, backward)  12.9 us
    another operation x1, loops' own time, local(): lax.fori_loop(0, STEPS // HALO_STEPS, one_block, (fields, empty_spectrum))  9.68 us
    mul x12, other arithmetic, yee_step(): (elec_y + factor * (backward_diff(magn_x, 1) - backward_diff(magn_z, 0)))...  8.82 us
    slice x92, local copies, waits for them, and re-layouts, forward_diff(): ahead = lax.slice_in_dim(field, 1, length, axis=along)  8.37 us
  transfers between devices with their start and end apart: 21, of which 12 were waited for; matrix products, arithmetic and copies ran while one was open for 2% of the time, Pallas kernels for 0%

profile of v1, /device:TPU:0, one launch (start us, length us, event | category | flops | bytes accessed | tf_op | source)
XLA Modules:
  0.0 412.0 jit_solution(7857703062916455113)
XLA Ops:
  11.0 3.4 select_bitcast_fusion.1
  14.5 2.5 select_bitcast_fusion
  17.0 2.4 collective-permute-start.4
  22.9 4.2 %collective-permute-start.6 = (f32[3,4,16,512]{3,2,1,0:T(8,128)S(1)}, f32[3,4,16,512]{3,2,1,0:T(8,128)S(1)}, u32[]{:S(2)}, u32[]{:S(2)}) collective-permute-start(f32[3,4,16,512]{3,2,1,0:T(8,128)S(1)} %get-tuple-element.239), channel_id=1, source_target_pairs={{0,1},{1,2},{2,3},{3,4},{4,5},{5,6},{6,7},{7,8},{8,9},{9,10},{10,1... | collective-permute-start | bytes 1179656 | tf_op jit(solution)/shard_map/ppermute | solution.py:25
  28.5 5.1 %cosine_multiply_fusion.1 = (f32[1,512,256]{2,1,0:T(8,128)}, f32[1,512,256]{2,1,0:T(8,128)}, f32[1,512,256]{2,1,0:T(8,128)}, f32[1,512,256]{2,1,0:T(8,128)}) fusion(s32[256]{0:T(256)S(1)} %iota_add_fusion), kind=kLoop, calls=%fused_computation.100 | loop fusion | flops 4456448 | bytes 2098176 | tf_op jit(solution)/shard_map/div | solution.py:101
  33.6 10.6 %collective-permute-done.6 = f32[3,4,16,512]{3,2,1,0:T(8,128)S(1)} collective-permute-done((f32[3,4,16,512]{3,2,1,0:T(8,128)S(1)}, f32[3,4,16,512]{3,2,1,0:T(8,128)S(1)}, u32[]{:S(2)}, u32[]{:S(2)}) %collective-permute-start.6) | collective-permute-done | bytes 393248 | tf_op jit(solution)/shard_map/ppermute | solution.py:25
  44.2 1.9 collective-permute-done.7
  46.6 234.1 %while.16 = (s32[]{:T(128)}, f32[6,6,8,512]{3,2,1,0:T(8,128)S(1)}, f32[2,2,2,6,512]{4,3,2,1,0:T(8,128)S(1)}, f32[14,16,512]{2,1,0:T(8,128)S(1)}, f32[14,16,512]{...) while((s32[]{:T(128)}, f32[6,6,8,512]{3,2,1,0:T(8,128)S(1)}, ...), condition=%wide.region_1.2_spmd.clone, body=%wide.region_0.1_spmd.clone.sunk | while | flops 24691188 | bytes 132281024 | solution.py:166
  48.2 3.1 collective-permute-start.1
  55.3 5.5 %collective-permute-start.3 = (f32[6,4,16,512]{3,2,1,0:T(8,128)S(1)}, f32[6,4,16,512]{3,2,1,0:T(8,128)}, u32[]{:S(2)}, u32[]{:S(2)}) collective-permute-start(f32[6,4,16,512]{3,2,1,0:T(8,128)S(1)} %get-tuple-element.359), channel_id=1, source_target_pairs={{0,1},{1,2},{2,3},{3,4},{4,5},{5,6},{6,7},{7,8},{8,9},{9,10},{10,1... | collective-permute-start | bytes 2359304 | tf_op jit(solution)/shard_map/while/body/eval_jaxpr/ppermute | solution.py:25
  61.6 15.0 %collective-permute-done.2 = f32[6,4,16,512]{3,2,1,0:T(8,128)} collective-permute-done((f32[6,4,16,512]{3,2,1,0:T(8,128)}, f32[6,4,16,512]{3,2,1,0:T(8,128)}, u32[]{:S(2)}, u32[]{:S(2)}) %collective-permute-start.2) | collective-permute-done | bytes 786464 | tf_op jit(solution)/shard_map/while/body/eval_jaxpr/ppermute | solution.py:28
  76.6 14.7 %collective-permute-done.3 = f32[6,4,16,512]{3,2,1,0:T(8,128)} collective-permute-done((f32[6,4,16,512]{3,2,1,0:T(8,128)S(1)}, f32[6,4,16,512]{3,2,1,0:T(8,128)}, u32[]{:S(2)}, u32[]{:S(2)}) %collective-permute-start.3) | collective-permute-done | bytes 786464 | tf_op jit(solution)/shard_map/while/body/eval_jaxpr/ppermute | solution.py:25
  91.3 1.8 pad_maximum_fusion.25
  104.8 3.1 collective-permute-start.1
  111.9 6.0 %collective-permute-start.3 = (f32[6,4,16,512]{3,2,1,0:T(8,128)S(1)}, f32[6,4,16,512]{3,2,1,0:T(8,128)}, u32[]{:S(2)}, u32[]{:S(2)}) collective-permute-start(f32[6,4,16,512]{3,2,1,0:T(8,128)S(1)} %get-tuple-element.359), channel_id=1, source_target_pairs={{0,1},{1,2},{2,3},{3,4},{4,5},{5,6},{6,7},{7,8},{8,9},{9,10},{10,1... | collective-permute-start | bytes 2359304 | tf_op jit(solution)/shard_map/while/body/eval_jaxpr/ppermute | solution.py:25
  118.9 15.0 %collective-permute-done.2 = f32[6,4,16,512]{3,2,1,0:T(8,128)} collective-permute-done((f32[6,4,16,512]{3,2,1,0:T(8,128)}, f32[6,4,16,512]{3,2,1,0:T(8,128)}, u32[]{:S(2)}, u32[]{:S(2)}) %collective-permute-start.2) | collective-permute-done | bytes 786464 | tf_op jit(solution)/shard_map/while/body/eval_jaxpr/ppermute | solution.py:28
  133.8 17.1 %collective-permute-done.3 = f32[6,4,16,512]{3,2,1,0:T(8,128)} collective-permute-done((f32[6,4,16,512]{3,2,1,0:T(8,128)S(1)}, f32[6,4,16,512]{3,2,1,0:T(8,128)}, u32[]{:S(2)}, u32[]{:S(2)}) %collective-permute-start.3) | collective-permute-done | bytes 786464 | tf_op jit(solution)/shard_map/while/body/eval_jaxpr/ppermute | solution.py:25
  151.0 1.8 pad_maximum_fusion.25
  164.5 3.1 collective-permute-start.1
  171.6 6.0 %collective-permute-start.3 = (f32[6,4,16,512]{3,2,1,0:T(8,128)S(1)}, f32[6,4,16,512]{3,2,1,0:T(8,128)}, u32[]{:S(2)}, u32[]{:S(2)}) collective-permute-start(f32[6,4,16,512]{3,2,1,0:T(8,128)S(1)} %get-tuple-element.359), channel_id=1, source_target_pairs={{0,1},{1,2},{2,3},{3,4},{4,5},{5,6},{6,7},{7,8},{8,9},{9,10},{10,1... | collective-permute-start | bytes 2359304 | tf_op jit(solution)/shard_map/while/body/eval_jaxpr/ppermute | solution.py:25
  178.5 15.0 %collective-permute-done.2 = f32[6,4,16,512]{3,2,1,0:T(8,128)} collective-permute-done((f32[6,4,16,512]{3,2,1,0:T(8,128)}, f32[6,4,16,512]{3,2,1,0:T(8,128)}, u32[]{:S(2)}, u32[]{:S(2)}) %collective-permute-start.2) | collective-permute-done | bytes 786464 | tf_op jit(solution)/shard_map/while/body/eval_jaxpr/ppermute | solution.py:28
  193.5 15.5 %collective-permute-done.3 = f32[6,4,16,512]{3,2,1,0:T(8,128)} collective-permute-done((f32[6,4,16,512]{3,2,1,0:T(8,128)S(1)}, f32[6,4,16,512]{3,2,1,0:T(8,128)}, u32[]{:S(2)}, u32[]{:S(2)}) %collective-permute-start.3) | collective-permute-done | bytes 786464 | tf_op jit(solution)/shard_map/while/body/eval_jaxpr/ppermute | solution.py:25
  209.0 1.8 pad_maximum_fusion.25
  222.5 3.1 collective-permute-start.1
  229.6 6.0 %collective-permute-start.3 = (f32[6,4,16,512]{3,2,1,0:T(8,128)S(1)}, f32[6,4,16,512]{3,2,1,0:T(8,128)}, u32[]{:S(2)}, u32[]{:S(2)}) collective-permute-start(f32[6,4,16,512]{3,2,1,0:T(8,128)S(1)} %get-tuple-element.359), channel_id=1, source_target_pairs={{0,1},{1,2},{2,3},{3,4},{4,5},{5,6},{6,7},{7,8},{8,9},{9,10},{10,1... | collective-permute-start | bytes 2359304 | tf_op jit(solution)/shard_map/while/body/eval_jaxpr/ppermute | solution.py:25
  236.5 15.0 %collective-permute-done.2 = f32[6,4,16,512]{3,2,1,0:T(8,128)} collective-permute-done((f32[6,4,16,512]{3,2,1,0:T(8,128)}, f32[6,4,16,512]{3,2,1,0:T(8,128)}, u32[]{:S(2)}, u32[]{:S(2)}) %collective-permute-start.2) | collective-permute-done | bytes 786464 | tf_op jit(solution)/shard_map/while/body/eval_jaxpr/ppermute | solution.py:28
  251.5 17.1 %collective-permute-done.3 = f32[6,4,16,512]{3,2,1,0:T(8,128)} collective-permute-done((f32[6,4,16,512]{3,2,1,0:T(8,128)S(1)}, f32[6,4,16,512]{3,2,1,0:T(8,128)}, u32[]{:S(2)}, u32[]{:S(2)}) %collective-permute-start.3) | collective-permute-done | bytes 786464 | tf_op jit(solution)/shard_map/while/body/eval_jaxpr/ppermute | solution.py:25
  268.6 1.8 pad_maximum_fusion.25
  280.9 2.3 all-gather
  283.4 1.8 fusion.14
  285.3 1.8 fusion.13
  293.4 110.3 %all-reduce.51.cloned.1.call-done = f32[96,2,2,2,256]{4,3,2,1,0:T(2,128)} async-done(((f32[96,2,2,2,256]{4,3,2,1,0:T(2,128)}), f32[96,2,2,2,256]{4,3,2,1,0:T(2,128)}) %all-reduce.51.cloned.1.call-update) | async-done | bytes 786448
  (371 shorter events, 73.5 us)
Async XLA Ops:
  7.2 396.6 %all-reduce.51.cloned.1.call-start = ((), (), s32[]{:S(2)}) async-start(), calls=%async_computation | async-start | bytes 1572864
  17.0 4.5 %collective-permute-start.4 = (f32[3,6,4,512]{3,2,1,0:T(4,128)S(1)}, f32[3,6,4,512]{3,2,1,0:T(4,128)S(1)}, u32[]{:S(2)}, u32[]{:S(2)}) collective-permute-start(f32[3,6,4,512]{3,2,1,0:T(4,128)S(1)} %get-tuple-element.241), channel_id=1, source_target_pairs={{0,16},{1,17},{2,18},{3,19},{4,20},{5,21},{6,22},{7,23},{8,24},{9,... | collective-permute-start | bytes 442376 | tf_op jit(solution)/shard_map/ppermute | solution.py:25
  19.4 3.3 collective-permute-start.5
  22.9 21.3 %collective-permute-start.6 = (f32[3,4,16,512]{3,2,1,0:T(8,128)S(1)}, f32[3,4,16,512]{3,2,1,0:T(8,128)S(1)}, u32[]{:S(2)}, u32[]{:S(2)}) collective-permute-start(f32[3,4,16,512]{3,2,1,0:T(8,128)S(1)} %get-tuple-element.239), channel_id=1, source_target_pairs={{0,1},{1,2},{2,3},{3,4},{4,5},{5,6},{6,7},{7,8},{8,9},{9,10},{10,1... | collective-permute-start | bytes 1179656 | tf_op jit(solution)/shard_map/ppermute | solution.py:25
  27.1 19.0 %collective-permute-start.7 = (f32[3,4,16,512]{3,2,1,0:T(8,128)S(1)}, f32[3,4,16,512]{3,2,1,0:T(8,128)S(1)}, u32[]{:S(2)}, u32[]{:S(2)}) collective-permute-start(f32[3,4,16,512]{3,2,1,0:T(8,128)S(1)} %get-tuple-element.240), channel_id=1, source_target_pairs={{1,0},{2,1},{3,2},{4,3},{5,4},{6,5},{7,6},{8,7},{9,8},{10,9},{11,1... | collective-permute-start | bytes 1179656 | tf_op jit(solution)/shard_map/ppermute | solution.py:28
  33.6 12.9 %copy-start.1 = (f32[6,6,8,512]{3,2,1,0:T(8,128)S(1)}, f32[6,6,8,512]{3,2,1,0:T(8,128)}, u32[]{:S(2)}) copy-start(f32[6,6,8,512]{3,2,1,0:T(8,128)} %param.7) | copy-start | bytes 1769476
  46.9 5.8 %collective-permute-start = (f32[6,6,4,512]{3,2,1,0:T(4,128)S(1)}, f32[6,6,4,512]{3,2,1,0:T(4,128)S(1)}, u32[]{:S(2)}, u32[]{:S(2)}) collective-permute-start(f32[6,6,4,512]{3,2,1,0:T(4,128)S(1)} %get-tuple-element.356), channel_id=1, source_target_pairs={{16,0},{17,1},{18,2},{19,3},{20,4},{21,5},{22,6},{23,7},{24,8},{25... | collective-permute-start | bytes 884744 | tf_op jit(solution)/shard_map/while/body/eval_jaxpr/ppermute | solution.py:28
  48.2 4.5 %collective-permute-start.1 = (f32[6,6,4,512]{3,2,1,0:T(4,128)S(1)}, f32[6,6,4,512]{3,2,1,0:T(4,128)S(1)}, u32[]{:S(2)}, u32[]{:S(2)}) collective-permute-start(f32[6,6,4,512]{3,2,1,0:T(4,128)S(1)} %get-tuple-element.357), channel_id=1, source_target_pairs={{0,16},{1,17},{2,18},{3,19},{4,20},{5,21},{6,22},{7,23},{8,24},{9,... | collective-permute-start | bytes 884744 | tf_op jit(solution)/shard_map/while/body/eval_jaxpr/ppermute | solution.py:25
  54.0 22.6 %collective-permute-start.2 = (f32[6,4,16,512]{3,2,1,0:T(8,128)}, f32[6,4,16,512]{3,2,1,0:T(8,128)}, u32[]{:S(2)}, u32[]{:S(2)}) collective-permute-start(f32[6,4,16,512]{3,2,1,0:T(8,128)} %get-tuple-element.358), channel_id=1, source_target_pairs={{1,0},{2,1},{3,2},{4,3},{5,4},{6,5},{7,6},{8,7},{9,8},{10,9},{11,1... | collective-permute-start | bytes 2359304 | tf_op jit(solution)/shard_map/while/body/eval_jaxpr/ppermute | solution.py:28
  55.3 36.0 %collective-permute-start.3 = (f32[6,4,16,512]{3,2,1,0:T(8,128)S(1)}, f32[6,4,16,512]{3,2,1,0:T(8,128)}, u32[]{:S(2)}, u32[]{:S(2)}) collective-permute-start(f32[6,4,16,512]{3,2,1,0:T(8,128)S(1)} %get-tuple-element.359), channel_id=1, source_target_pairs={{0,1},{1,2},{2,3},{3,4},{4,5},{5,6},{6,7},{7,8},{8,9},{9,10},{10,1... | collective-permute-start | bytes 2359304 | tf_op jit(solution)/shard_map/while/body/eval_jaxpr/ppermute | solution.py:25
  103.5 5.8 %collective-permute-start = (f32[6,6,4,512]{3,2,1,0:T(4,128)S(1)}, f32[6,6,4,512]{3,2,1,0:T(4,128)S(1)}, u32[]{:S(2)}, u32[]{:S(2)}) collective-permute-start(f32[6,6,4,512]{3,2,1,0:T(4,128)S(1)} %get-tuple-element.356), channel_id=1, source_target_pairs={{16,0},{17,1},{18,2},{19,3},{20,4},{21,5},{22,6},{23,7},{24,8},{25... | collective-permute-start | bytes 884744 | tf_op jit(solution)/shard_map/while/body/eval_jaxpr/ppermute | solution.py:28
  104.8 4.5 %collective-permute-start.1 = (f32[6,6,4,512]{3,2,1,0:T(4,128)S(1)}, f32[6,6,4,512]{3,2,1,0:T(4,128)S(1)}, u32[]{:S(2)}, u32[]{:S(2)}) collective-permute-start(f32[6,6,4,512]{3,2,1,0:T(4,128)S(1)} %get-tuple-element.357), channel_id=1, source_target_pairs={{0,16},{1,17},{2,18},{3,19},{4,20},{5,21},{6,22},{7,23},{8,24},{9,... | collective-permute-start | bytes 884744 | tf_op jit(solution)/shard_map/while/body/eval_jaxpr/ppermute | solution.py:25
  110.6 23.2 %collective-permute-start.2 = (f32[6,4,16,512]{3,2,1,0:T(8,128)}, f32[6,4,16,512]{3,2,1,0:T(8,128)}, u32[]{:S(2)}, u32[]{:S(2)}) collective-permute-start(f32[6,4,16,512]{3,2,1,0:T(8,128)} %get-tuple-element.358), channel_id=1, source_target_pairs={{1,0},{2,1},{3,2},{4,3},{5,4},{6,5},{7,6},{8,7},{9,8},{10,9},{11,1... | collective-permute-start | bytes 2359304 | tf_op jit(solution)/shard_map/while/body/eval_jaxpr/ppermute | solution.py:28
  111.9 39.0 %collective-permute-start.3 = (f32[6,4,16,512]{3,2,1,0:T(8,128)S(1)}, f32[6,4,16,512]{3,2,1,0:T(8,128)}, u32[]{:S(2)}, u32[]{:S(2)}) collective-permute-start(f32[6,4,16,512]{3,2,1,0:T(8,128)S(1)} %get-tuple-element.359), channel_id=1, source_target_pairs={{0,1},{1,2},{2,3},{3,4},{4,5},{5,6},{6,7},{7,8},{8,9},{9,10},{10,1... | collective-permute-start | bytes 2359304 | tf_op jit(solution)/shard_map/while/body/eval_jaxpr/ppermute | solution.py:25
  163.2 5.8 %collective-permute-start = (f32[6,6,4,512]{3,2,1,0:T(4,128)S(1)}, f32[6,6,4,512]{3,2,1,0:T(4,128)S(1)}, u32[]{:S(2)}, u32[]{:S(2)}) collective-permute-start(f32[6,6,4,512]{3,2,1,0:T(4,128)S(1)} %get-tuple-element.356), channel_id=1, source_target_pairs={{16,0},{17,1},{18,2},{19,3},{20,4},{21,5},{22,6},{23,7},{24,8},{25... | collective-permute-start | bytes 884744 | tf_op jit(solution)/shard_map/while/body/eval_jaxpr/ppermute | solution.py:28
  164.5 4.5 %collective-permute-start.1 = (f32[6,6,4,512]{3,2,1,0:T(4,128)S(1)}, f32[6,6,4,512]{3,2,1,0:T(4,128)S(1)}, u32[]{:S(2)}, u32[]{:S(2)}) collective-permute-start(f32[6,6,4,512]{3,2,1,0:T(4,128)S(1)} %get-tuple-element.357), channel_id=1, source_target_pairs={{0,16},{1,17},{2,18},{3,19},{4,20},{5,21},{6,22},{7,23},{8,24},{9,... | collective-permute-start | bytes 884744 | tf_op jit(solution)/shard_map/while/body/eval_jaxpr/ppermute | solution.py:25
  170.3 23.2 %collective-permute-start.2 = (f32[6,4,16,512]{3,2,1,0:T(8,128)}, f32[6,4,16,512]{3,2,1,0:T(8,128)}, u32[]{:S(2)}, u32[]{:S(2)}) collective-permute-start(f32[6,4,16,512]{3,2,1,0:T(8,128)} %get-tuple-element.358), channel_id=1, source_target_pairs={{1,0},{2,1},{3,2},{4,3},{5,4},{6,5},{7,6},{8,7},{9,8},{10,9},{11,1... | collective-permute-start | bytes 2359304 | tf_op jit(solution)/shard_map/while/body/eval_jaxpr/ppermute | solution.py:28
  171.6 37.4 %collective-permute-start.3 = (f32[6,4,16,512]{3,2,1,0:T(8,128)S(1)}, f32[6,4,16,512]{3,2,1,0:T(8,128)}, u32[]{:S(2)}, u32[]{:S(2)}) collective-permute-start(f32[6,4,16,512]{3,2,1,0:T(8,128)S(1)} %get-tuple-element.359), channel_id=1, source_target_pairs={{0,1},{1,2},{2,3},{3,4},{4,5},{5,6},{6,7},{7,8},{8,9},{9,10},{10,1... | collective-permute-start | bytes 2359304 | tf_op jit(solution)/shard_map/while/body/eval_jaxpr/ppermute | solution.py:25
  221.2 5.8 %collective-permute-start = (f32[6,6,4,512]{3,2,1,0:T(4,128)S(1)}, f32[6,6,4,512]{3,2,1,0:T(4,128)S(1)}, u32[]{:S(2)}, u32[]{:S(2)}) collective-permute-start(f32[6,6,4,512]{3,2,1,0:T(4,128)S(1)} %get-tuple-element.356), channel_id=1, source_target_pairs={{16,0},{17,1},{18,2},{19,3},{20,4},{21,5},{22,6},{23,7},{24,8},{25... | collective-permute-start | bytes 884744 | tf_op jit(solution)/shard_map/while/body/eval_jaxpr/ppermute | solution.py:28
  222.5 4.5 %collective-permute-start.1 = (f32[6,6,4,512]{3,2,1,0:T(4,128)S(1)}, f32[6,6,4,512]{3,2,1,0:T(4,128)S(1)}, u32[]{:S(2)}, u32[]{:S(2)}) collective-permute-start(f32[6,6,4,512]{3,2,1,0:T(4,128)S(1)} %get-tuple-element.357), channel_id=1, source_target_pairs={{0,16},{1,17},{2,18},{3,19},{4,20},{5,21},{6,22},{7,23},{8,24},{9,... | collective-permute-start | bytes 884744 | tf_op jit(solution)/shard_map/while/body/eval_jaxpr/ppermute | solution.py:25
  228.3 23.2 %collective-permute-start.2 = (f32[6,4,16,512]{3,2,1,0:T(8,128)}, f32[6,4,16,512]{3,2,1,0:T(8,128)}, u32[]{:S(2)}, u32[]{:S(2)}) collective-permute-start(f32[6,4,16,512]{3,2,1,0:T(8,128)} %get-tuple-element.358), channel_id=1, source_target_pairs={{1,0},{2,1},{3,2},{4,3},{5,4},{6,5},{7,6},{8,7},{9,8},{10,9},{11,1... | collective-permute-start | bytes 2359304 | tf_op jit(solution)/shard_map/while/body/eval_jaxpr/ppermute | solution.py:28
  229.6 39.0 %collective-permute-start.3 = (f32[6,4,16,512]{3,2,1,0:T(8,128)S(1)}, f32[6,4,16,512]{3,2,1,0:T(8,128)}, u32[]{:S(2)}, u32[]{:S(2)}) collective-permute-start(f32[6,4,16,512]{3,2,1,0:T(8,128)S(1)} %get-tuple-element.359), channel_id=1, source_target_pairs={{0,1},{1,2},{2,3},{3,4},{4,5},{5,6},{6,7},{7,8},{8,9},{9,10},{10,1... | collective-permute-start | bytes 2359304 | tf_op jit(solution)/shard_map/while/body/eval_jaxpr/ppermute | solution.py:25
  280.7 7.7 %copy-start = (f32[6,6,8,512]{3,2,1,0:T(8,128)}, f32[6,6,8,512]{3,2,1,0:T(8,128)S(1)}, u32[]{:S(2)}) copy-start(f32[6,6,8,512]{3,2,1,0:T(8,128)S(1)} %get-tuple-element.168) | copy-start | bytes 1769476
  280.7 6.4 %copy-start.4 = (f32[1,512,256]{2,1,0:T(8,128)S(1)}, f32[1,512,256]{2,1,0:T(8,128)}, u32[]{:S(2)}) copy-start(f32[1,512,256]{2,1,0:T(8,128)} %get-tuple-element.247) | copy-start | bytes 1572868
  280.7 6.4 %copy-start.5 = (f32[1,512,256]{2,1,0:T(8,128)S(1)}, f32[1,512,256]{2,1,0:T(8,128)}, u32[]{:S(2)}) copy-start(f32[1,512,256]{2,1,0:T(8,128)} %get-tuple-element.248) | copy-start | bytes 1572868
  280.7 7.0 %copy-start.2 = (f32[1,512,256]{2,1,0:T(8,128)S(1)}, f32[1,512,256]{2,1,0:T(8,128)}, u32[]{:S(2)}) copy-start(f32[1,512,256]{2,1,0:T(8,128)} %get-tuple-element.245) | copy-start | bytes 1572868
  280.8 7.0 %copy-start.3 = (f32[1,512,256]{2,1,0:T(8,128)S(1)}, f32[1,512,256]{2,1,0:T(8,128)}, u32[]{:S(2)}) copy-start(f32[1,512,256]{2,1,0:T(8,128)} %get-tuple-element.246) | copy-start | bytes 1572868
  280.9 7.6 %copy-start.8 = (f32[1,96,6]{1,2,0:T(8,128)S(1)}, f32[1,96,6]{1,2,0:T(8,128)}, u32[]{:S(2)}) copy-start(f32[1,96,6]{1,2,0:T(8,128)} %get-tuple-element.251) | copy-start | bytes 6916
  280.9 7.6 %copy-start.9 = (f32[1,96,6]{1,2,0:T(8,128)S(1)}, f32[1,96,6]{1,2,0:T(8,128)}, u32[]{:S(2)}) copy-start(f32[1,96,6]{1,2,0:T(8,128)} %get-tuple-element.252) | copy-start | bytes 6916
  283.4 6.1 %copy-start.6 = (f32[1,96,6]{1,2,0:T(8,128)S(1)}, f32[1,96,6]{1,2,0:T(8,128)}, u32[]{:S(2)}) copy-start(f32[1,96,6]{1,2,0:T(8,128)} %get-tuple-element.249) | copy-start | bytes 6916
  283.4 6.1 %copy-start.7 = (f32[1,96,6]{1,2,0:T(8,128)S(1)}, f32[1,96,6]{1,2,0:T(8,128)}, u32[]{:S(2)}) copy-start(f32[1,96,6]{1,2,0:T(8,128)} %get-tuple-element.250) | copy-start | bytes 6916
  289.5 2.6 copy-start.10
Sparse Core Ops, SparseCore 0:
  292.2 111.4 all-reduce.50
